TPU v7x, 32 devices: a whole 2x2x4 slice. The times are simulated.
32 devices in a mesh: head: 2 (over y), seq: 16 (over z, x, core).
Axes of the slice: x: 2, y: 2, z: 4, core: 2. Of those that a mesh axis runs over, the one named last changes fastest.
Arguments:
- latent_q: bfloat16 [32, 128, 576], P(None, 'head'), may hold values from -13 to 13
- latent_keys: bfloat16 [16384, 576], P('seq'), may hold values from -10 to 10
- idx_q: bfloat16 [32, 64, 128], replicated, may hold values from -1.5 to 1.5
- idx_keys: bfloat16 [16, 1024, 128], P('seq', 'head'), may hold values from -1.5 to 1.5
- idx_weight: bfloat16 [32, 64], replicated, may hold values from -1.8 to 1.8
Outputs:
- loss: float32 [], replicated
- query_grad: float32 [2048, 128], P(('head', 'seq'))
- weight_grad: float32 [2048], P(('head', 'seq'))
- key_grad: float32 [16, 1024, 128], P('seq', 'head')
All inputs are finite; a program needn't handle non-finite values.
Results may differ from a plain program's by a relative error of at most 0.0027.
Values may be sent and summed in bfloat16 or wider, within the bound.
A program may use at most 64 MiB of HBM per device.

v0:
```python
import functools
import math

import jax
import jax.numpy as jnp
from jax import lax
from jax.experimental import pallas as pl
from jax.experimental.pallas import tpu as pltpu
from jax.sharding import PartitionSpec as P

MESH = pl.DeviceIdType.MESH
NT = (((1,), (1,)), ((), ()))
TN = (((0,), (0,)), ((), ()))
F32 = jnp.float32
BF16 = jnp.bfloat16

exponent_scale = 192 ** (-0.5) * math.log2(math.e)


def to_row(column):
    wide = jnp.broadcast_to(column, (column.shape[0], 128))
    copies = 128 // column.shape[0]
    return jnp.concatenate([wide] * copies, axis=0).T[0:1, :]


def to_column(row, count):
    return jnp.broadcast_to(row, (128, 128)).T[0:count, 0:1]


def join_log2(values):
    top = jnp.max(values, axis=0)
    return top + jnp.log2(jnp.sum(jnp.exp2(values - top[None]), axis=0))


def join_log(values):
    top = jnp.max(values, axis=0)
    return top + jnp.log(jnp.sum(jnp.exp(values - top[None]), axis=0))


def kernel(
    heads_axis, seq_axis, heads, queries_count,
    latent_q, turned_keys, query_ref, keys_ref, weight_ref,
    loss_out, query_out, prod_out, key_out,
    latent_keys, idx_q, flat_queries, weights, own_term, pair_recv, index_all, expo, base, stat_all, sum_send, sum_recv, act, dact, term, term_recv, loss_all,
    stat_send_sem, stat_recv_sem, sum_send_sem, sum_recv_sem,
    term_send_sem, term_recv_sem, loss_send_sem, loss_recv_sem, pair_send_sem, pair_recv_sem, index_send_sem, index_recv_sem,
):
    my_head = lax.axis_index("head")
    my_seq = lax.axis_index("seq")
    devices = heads_axis * seq_axis
    me = my_head * seq_axis + my_seq
    barrier = pltpu.get_barrier_semaphore()

    def place(index):
        return (index // seq_axis, lax.rem(index, seq_axis))

    def greet(offset, carry):
        other = lax.rem(me + offset, devices)
        pl.semaphore_signal(barrier, inc=1, device_id=place(other), device_id_type=MESH)
        return carry

    lax.fori_loop(1, devices, greet, 0)

    rows, width = latent_q.shape
    local_heads = rows // queries_count
    step = 256
    latent_keys[...] = turned_keys[...].T

    def attend(i, carry):
        columns = pl.ds(pl.multiple_of(i * step, step), step)
        scores = lax.dot_general(
            latent_keys[...], latent_q[columns, :], NT, preferred_element_type=F32
        )
        top = jnp.max(scores, axis=0, keepdims=True)
        part = jnp.exp2((scores - top) * exponent_scale)
        expo[:, columns] = part.astype(BF16)
        total = jnp.sum(part, axis=0, keepdims=True)
        base[:, columns] = top * exponent_scale
        stat_all[my_seq, :, columns] = top * exponent_scale + jnp.log2(total)
        return carry

    lax.fori_loop(0, rows // step, attend, 0)

    pl.semaphore_wait(barrier, devices - 1)

    def stat_copy(offset, source, target):
        return pltpu.make_async_remote_copy(
            src_ref=stat_all.at[source],
            dst_ref=stat_all.at[source],
            send_sem=stat_send_sem.at[offset],
            recv_sem=stat_recv_sem.at[source],
            device_id=(my_head, target),
            device_id_type=MESH,
        )

    def stat_start(offset, carry):
        stat_copy(offset, my_seq, lax.rem(my_seq + offset, seq_axis)).start()
        return carry

    def stat_wait(offset, carry):
        other = lax.rem(my_seq + offset, seq_axis)
        stat_copy(offset, other, other).wait_recv()
        return carry

    def stat_sent(offset, carry):
        stat_copy(offset, my_seq, lax.rem(my_seq + offset, seq_axis)).wait_send()
        return carry

    def index_copy(offset, source, target):
        return pltpu.make_async_remote_copy(
            src_ref=index_all.at[source],
            dst_ref=index_all.at[source],
            send_sem=index_send_sem.at[offset],
            recv_sem=index_recv_sem.at[source],
            device_id=(my_head, target),
            device_id_type=MESH,
        )

    def index_start(offset, carry):
        index_copy(offset, my_seq, lax.rem(my_seq + offset, seq_axis)).start()
        return carry

    def index_wait(offset, carry):
        other = lax.rem(my_seq + offset, seq_axis)
        index_copy(offset, other, other).wait_recv()
        return carry

    def index_sent(offset, carry):
        index_copy(offset, my_seq, lax.rem(my_seq + offset, seq_axis)).wait_send()
        return carry

    lax.fori_loop(1, seq_axis, stat_start, 0)

    blocks, block, _ = weights.shape
    fine = keys_ref.shape[0]
    group = math.gcd(blocks, 8)
    heads_in_block = block // queries_count
    wide = weight_ref[...].astype(F32)
    flat_queries[...] = query_ref[...].astype(F32)
    index_heads = wide.shape[1]
    for g in range(wide.shape[1]):
        row = g % heads_in_block * queries_count
        weights[g // heads_in_block, row : row + queries_count, :] = wide[:, g : g + 1]
        picked = flat_queries[pl.ds(g, queries_count, stride=index_heads), :]
        idx_q[g // heads_in_block, row : row + queries_count, :] = picked.astype(BF16)

    def index_scores(i, logits):
        queries = idx_q[pl.ds(i * group, group)]
        part = lax.dot_general(
            queries.reshape(group * block, -1), keys_ref[...], NT, preferred_element_type=F32
        )
        part = part.reshape(group, block, fine)
        act[pl.ds(i * group, group)] = part
        weighted = weights[pl.ds(i * group, group)] * jnp.maximum(part, 0.0)
        return logits + jnp.sum(
            weighted.reshape(group * heads_in_block, queries_count, fine), axis=0
        )

    logits = lax.fori_loop(
        0, blocks // group, index_scores, jnp.zeros((queries_count, fine), F32)
    )
    index_top = jnp.max(logits, axis=1, keepdims=True)
    index_total = jnp.sum(jnp.exp(logits - index_top), axis=1, keepdims=True)
    index_all[my_seq] = to_row(index_top + jnp.log(index_total))

    lax.fori_loop(1, seq_axis, index_start, 0)
    lax.fori_loop(1, seq_axis, stat_wait, 0)
    lax.fori_loop(1, seq_axis, index_wait, 0)

    joined = join_log2(stat_all[...])
    factor = jnp.exp2(base[...] - joined)
    upper = factor.astype(BF16).astype(F32)
    lower = factor - upper
    place_q = lax.broadcasted_iota(jnp.int32, (128, rows), 0)
    start = lax.broadcasted_iota(jnp.int32, (128, rows), 1)
    first = place_q * local_heads
    second = (place_q - queries_count) * local_heads
    in_first = jnp.logical_and(start >= first, start < first + local_heads)
    in_second = jnp.logical_and(start >= second, start < second + local_heads)
    spread = jnp.where(in_first, upper, jnp.where(in_second, lower, 0.0)).astype(BF16)
    summed = lax.dot_general(expo[...], spread, NT, preferred_element_type=F32).T
    summed = summed[0:queries_count] + summed[queries_count : 2 * queries_count]
    index_row = join_log(index_all[...])
    for j in range(heads_axis):
        sum_send[j, 0:queries_count, :] = summed[:, j * fine : (j + 1) * fine]
        sum_send[j, queries_count : queries_count + 1, 0:128] = index_row

    def sum_copy(offset, block_index, slot, target):
        return pltpu.make_async_remote_copy(
            src_ref=sum_send.at[block_index],
            dst_ref=sum_recv.at[slot],
            send_sem=sum_send_sem.at[offset],
            recv_sem=sum_recv_sem.at[slot],
            device_id=(target, my_seq),
            device_id_type=MESH,
        )

    for offset in range(1, heads_axis):
        target = lax.rem(my_head + offset, heads_axis)
        sum_copy(offset, target, my_head, target).start()
    targets = sum_send[my_head, 0:queries_count, :]
    index_rows = [index_row]
    for offset in range(1, heads_axis):
        source = lax.rem(my_head + offset, heads_axis)
        sum_copy(offset, source, source, source).wait_recv()
        targets = targets + sum_recv[source, 0:queries_count, :]
        index_rows.append(sum_recv[source, queries_count : queries_count + 1, 0:128])
    targets = targets / heads
    index_log = to_column(join_log(jnp.stack(index_rows)), queries_count)
    shifted = logits - index_log
    positive = targets > 0
    own_loss = jnp.where(positive, targets * jnp.log(jnp.where(positive, targets, 1.0)), 0.0)
    own_loss = jnp.sum(own_loss - targets * shifted, axis=0, keepdims=True)
    own_loss = sum(own_loss[:, i * 128 : (i + 1) * 128] for i in range(fine // 128))
    grad = jnp.exp(shifted) - targets
    loss_all[me] = own_loss

    def loss_copy(offset, slot, target):
        return pltpu.make_async_remote_copy(
            src_ref=loss_all.at[slot],
            dst_ref=loss_all.at[slot],
            send_sem=loss_send_sem.at[offset],
            recv_sem=loss_recv_sem.at[slot],
            device_id=place(target),
            device_id_type=MESH,
        )

    chunk = term.shape[1]
    owners = block // chunk

    def term_copy(source_slot, slot, target):
        return pltpu.make_async_remote_copy(
            src_ref=term.at[source_slot],
            dst_ref=term_recv.at[slot],
            send_sem=term_send_sem.at[source_slot],
            recv_sem=term_recv_sem.at[slot],
            device_id=place(target),
            device_id_type=MESH,
        )

    grads = jnp.concatenate([grad] * heads_in_block, axis=0)
    grad_upper = grads.astype(BF16).astype(F32)
    grad_lower = grads - grad_upper

    my_block = me // owners
    parity = lax.rem(my_seq, 2)
    pair = my_seq + 1 - 2 * parity

    def pair_copy(owner):
        return pltpu.make_async_remote_copy(
            src_ref=own_term.at[owner],
            dst_ref=pair_recv.at[owner],
            send_sem=pair_send_sem.at[owner],
            recv_sem=pair_recv_sem.at[owner],
            device_id=(my_head, pair),
            device_id_type=MESH,
        )

    def back(b):
        part = act[b]
        on = part > 0
        dact[b] = jnp.where(on, grads * weights[b], 0.0).astype(BF16)
        both = jnp.concatenate(
            [jnp.where(on, grad_upper, 0.0), jnp.where(on, grad_lower, 0.0)], axis=0
        ).astype(BF16)
        result = jnp.dot(both, keys_ref[...], preferred_element_type=F32)
        result = result[0:block] + result[block : 2 * block]
        for j in range(owners):
            own_term[b * owners + j] = result[j * chunk : (j + 1) * chunk]

    def finish(owner):
        pair_copy(owner).wait_recv()
        term[owner] = (own_term[owner] + pair_recv[owner]).astype(BF16)

        @pl.when(owner != me)
        def _():
            term_copy(owner, me, owner).start()

    half = devices // 2

    def partner_owner(offset):
        return lax.rem(2 * (me // 2 + offset), devices) + 1 - parity

    def kept_owner(offset):
        return lax.rem(2 * (me // 2 + offset), devices) + parity

    if owners == 1:

        def first_half(offset, carry):
            back(partner_owner(offset))
            pair_copy(partner_owner(offset)).start()
            return carry

        def second_half(offset, carry):
            back(kept_owner(offset))
            finish(kept_owner(offset))
            return carry

        lax.fori_loop(1, half + 1, first_half, 0)
        lax.fori_loop(1, half + 1, second_half, 0)
    else:

        def every_block(b, carry):
            back(b)
            return carry

        def pair_start(offset, carry):
            pair_copy(partner_owner(offset)).start()
            return carry

        def finish_all(offset, carry):
            finish(kept_owner(offset))
            return carry

        lax.fori_loop(0, blocks, every_block, 0)
        lax.fori_loop(1, half + 1, pair_start, 0)
        lax.fori_loop(1, half + 1, finish_all, 0)

    def loss_start(offset, carry):
        loss_copy(offset, me, lax.rem(me + offset, devices)).start()
        return carry

    lax.fori_loop(1, devices, loss_start, 0)

    key_out[...] = lax.dot_general(
        dact[...].reshape(blocks * block, fine),
        idx_q[...].reshape(blocks * block, -1),
        TN,
        preferred_element_type=F32,
    )

    def term_wait(offset, total):
        source = kept_owner(offset)
        term_copy(source, source, source).wait_recv()
        return total + term_recv[source].astype(F32)

    total = lax.fori_loop(1, half, term_wait, own_term[me] + pair_recv[me])
    own_block = my_block
    inner = me - my_block * owners
    own_weights = weights[own_block]
    own_queries = idx_q[own_block].astype(F32)
    if owners == 1:
        query_out[...] = total * own_weights
        prod_out[...] = total * own_queries
    else:
        for j in range(owners):

            @pl.when(inner == j)
            def _():
                query_out[...] = total * own_weights[j * chunk : (j + 1) * chunk]
                prod_out[...] = total * own_queries[j * chunk : (j + 1) * chunk]

    def loss_wait(offset, carry):
        source = lax.rem(me + offset, devices)
        loss_copy(offset, source, source).wait_recv()
        return carry

    lax.fori_loop(1, devices, loss_wait, 0)
    loss_out[...] = jnp.sum(loss_all[...], axis=0)

    lax.fori_loop(1, seq_axis, stat_sent, 0)
    lax.fori_loop(1, seq_axis, index_sent, 0)
    for offset in range(1, heads_axis):
        target = lax.rem(my_head + offset, heads_axis)
        sum_copy(offset, target, my_head, target).wait_send()

    def last_sent(offset, carry):
        other = lax.rem(me + offset, devices)
        loss_copy(offset, me, other).wait_send()
        return carry

    def half_sent(offset, carry):
        term_copy(kept_owner(offset), me, kept_owner(offset)).wait_send()
        return carry

    def pair_sent(offset, carry):
        pair_copy(partner_owner(offset)).wait_send()
        return carry

    lax.fori_loop(1, devices, last_sent, 0)
    lax.fori_loop(1, half, half_sent, 0)
    lax.fori_loop(1, half + 1, pair_sent, 0)


def closing(queries_count, loss_in, query_in, prod_in, key_in, loss_out, query_out, weight_out, key_out):
    loss_out[...] = jnp.sum(loss_in[...], axis=1, keepdims=True) / queries_count
    query_out[...] = query_in[...]
    ones = jnp.ones((8, prod_in.shape[1]), F32)
    sums = lax.dot_general(
        ones, prod_in[...], NT, precision=lax.Precision.HIGHEST, preferred_element_type=F32
    )
    weight_out[...] = sums[0:1]
    key_out[...] = key_in[...]


def shards(heads_axis, seq_axis, latent_q, latent_keys, idx_q, idx_keys, idx_weight):
    queries_count, local_heads, width = latent_q.shape
    index_heads, size = idx_q.shape[1:]
    rows = queries_count * local_heads
    keys = latent_keys.shape[0]
    fine = idx_keys.shape[1]
    devices = heads_axis * seq_axis
    all_rows = queries_count * index_heads
    chunk = all_rows // devices
    block = max(chunk, queries_count)
    blocks = all_rows // block
    queries = idx_q.reshape(all_rows, size)
    vmem = pl.BlockSpec(memory_space=pltpu.VMEM)
    dma = pltpu.SemaphoreType.DMA
    loss, query_grad, prod, key_grad = pl.pallas_call(
        functools.partial(
            kernel, heads_axis, seq_axis, local_heads * heads_axis, queries_count
        ),
        out_shape=(
            jax.ShapeDtypeStruct((1, 128), F32),
            jax.ShapeDtypeStruct((chunk, size), F32),
            jax.ShapeDtypeStruct((chunk, size), F32),
            jax.ShapeDtypeStruct((fine, size), F32),
        ),
        in_specs=[vmem] * 5,
        out_specs=(vmem,) * 4,
        scratch_shapes=[
            pltpu.VMEM((keys, width), BF16),
            pltpu.VMEM((blocks, block, size), BF16),
            pltpu.VMEM((all_rows, size), F32),
            pltpu.VMEM((blocks, block, 1), F32),
            pltpu.VMEM((devices, chunk, size), F32),
            pltpu.VMEM((devices, chunk, size), F32),
            pltpu.VMEM((seq_axis, 1, 128), F32),
            pltpu.VMEM((keys, rows), BF16),
            pltpu.VMEM((1, rows), F32),
            pltpu.VMEM((seq_axis, 1, rows), F32),
            pltpu.VMEM((heads_axis, queries_count + 8, fine), F32),
            pltpu.VMEM((heads_axis, queries_count + 8, fine), F32),
            pltpu.VMEM((blocks, block, fine), F32),
            pltpu.VMEM((blocks, block, fine), BF16),
            pltpu.VMEM((devices, chunk, size), BF16),
            pltpu.VMEM((devices, chunk, size), BF16),
            pltpu.VMEM((devices, 1, 128), F32),
            dma((seq_axis,)),
            dma((seq_axis,)),
            dma((heads_axis,)),
            dma((heads_axis,)),
            dma((devices,)),
            dma((devices,)),
            dma((devices,)),
            dma((devices,)),
            dma((devices,)),
            dma((devices,)),
            dma((seq_axis,)),
            dma((seq_axis,)),
        ],
        compiler_params=pltpu.CompilerParams(
            collective_id=0, has_side_effects=True, vmem_limit_bytes=60 * 1024 * 1024
        ),
    )(latent_q.reshape(rows, width), latent_keys.T, queries, idx_keys[0], idx_weight)
    loss, query_grad, weight_grad, key_grad = pl.pallas_call(
        functools.partial(closing, queries_count),
        out_shape=(
            jax.ShapeDtypeStruct((1, 1), F32),
            jax.ShapeDtypeStruct((chunk, size), F32),
            jax.ShapeDtypeStruct((1, chunk), F32),
            jax.ShapeDtypeStruct((fine, size), F32),
        ),
        in_specs=[vmem] * 4,
        out_specs=(vmem,) * 4,
    )(loss, query_grad, prod, key_grad)
    return (loss.reshape(()), query_grad, weight_grad.reshape(-1), key_grad[None])


def solution(mesh):
    in_specs = (P(None, "head", None), P("seq", None), P(), P("seq", "head", None), P())
    out_specs = (P(), P(("head", "seq"), None), P(("head", "seq")), P("seq", "head", None))
    body = functools.partial(shards, mesh.shape["head"], mesh.shape["seq"])
    return jax.shard_map(body, mesh=mesh, in_specs=in_specs, out_specs=out_specs, check_vma=False)
```

profile of v0, /device:TPU:0, one launch (start us, length us, event | category | flops | bytes accessed | tf_op | source)
XLA Modules:
  0.0 42.3 jit_solution(17021850044341978943)
XLA Ops:
  0.6 39.9 %shard_map.84 = (f32[1,128]{1,0:T(1,128)}, f32[64,128]{1,0:T(8,128)}, f32[64,128]{1,0:T(8,128)}, f32[512,128]{1,0:T(8,128)}) custom-call(bf16[2048,576]{1,0:T(8,128)(2,1)} %bitcast.7, bf16[576,1024]{1,0:T(8,128)(2,1)} %bitcast.8, bf16[2048,128]{1,0:T(8,128)(2,1)} %bitcast.9, bf16[512,128]{1,0:T(8,128)(2,1)} %bitcast.10, bf16[32,64]{1,0:T(8,128)(2,1)} %weight_ref.1), custom_call_target="tpu_custom_call" | custom-call | tf_op jit(solution)/shard_map/pallas_call | solution.py:410
  40.5 1.8 %shard_map.85 = (f32[1,1]{1,0:T(1,128)}, f32[64,128]{1,0:T(8,128)}, f32[1,64]{1,0:T(1,128)}, f32[512,128]{1,0:T(8,128)}) custom-call(f32[1,128]{1,0:T(1,128)} %get-tuple-element.12.loss_in, f32[64,128]{1,0:T(8,128)} %get-tuple-element.13.query_in, f32[64,128]{1,0:T(8,128)} %get-tuple-element.14.prod_in, f32[512,128]{1,0:T(8,128)} %get-tuple-element.15.key_in), custom_call_target="tpu_custom_call" | custom-call | tf_op jit(solution)/shard_map/pallas_call | solution.py:457
where the time goes:
time: 42.5 us; the launch traced here: 42.3 us
  Pallas kernels  41.7 us (98%)
  between operations  0.64 us (2%)
    pallas_call x1, Pallas kernels, shards(): pl.pallas_call(functools.partial(kernel, heads_axis, seq_axis, local_head...  39.9 us
    pallas_call x1, Pallas kernels, shards(): pl.pallas_call(functools.partial(closing, queries_count), out_shape=(jax....  1.78 us

commit v1 on v0

v1 whole, which is shorter than its diff:
```python
import functools
import math

import jax
import jax.numpy as jnp
from jax import lax
from jax.experimental import pallas as pl
from jax.experimental.pallas import tpu as pltpu
from jax.sharding import PartitionSpec as P

MESH = pl.DeviceIdType.MESH
NT = (((1,), (1,)), ((), ()))
TN = (((0,), (0,)), ((), ()))
F32 = jnp.float32
BF16 = jnp.bfloat16

exponent_scale = 192 ** (-0.5) * math.log2(math.e)


def to_row(column):
    wide = jnp.broadcast_to(column, (column.shape[0], 128))
    copies = 128 // column.shape[0]
    return jnp.concatenate([wide] * copies, axis=0).T[0:1, :]


def to_column(row, count):
    return jnp.broadcast_to(row, (128, 128)).T[0:count, 0:1]


def join_log2(values):
    top = jnp.max(values, axis=0)
    return top + jnp.log2(jnp.sum(jnp.exp2(values - top[None]), axis=0))


def join_log(values):
    top = jnp.max(values, axis=0)
    return top + jnp.log(jnp.sum(jnp.exp(values - top[None]), axis=0))


def kernel(
    heads_axis, seq_axis, heads, queries_count,
    latent_q_hbm, turned_keys_hbm, query_hbm, keys_hbm, weight_hbm,
    loss_out, query_out, prod_out, key_out,
    latent_q, turned_keys, query_ref, keys_ref, weight_ref, load_sem,
    latent_keys, scores_a, scores_b, top_a, top_b,
    idx_q, flat_queries, weights, own_term, pair_recv, index_all, expo, base, spread, stat_all, sum_send, sum_recv, act, dact, term_a, recv_a, term_b, recv_b, loss_all,
    stat_send_sem, stat_recv_sem, sum_send_sem, sum_recv_sem,
    a_send_sem, a_recv_sem, b_send_sem, b_recv_sem, loss_send_sem, loss_recv_sem, pair_send_sem, pair_recv_sem, index_send_sem, index_recv_sem,
):
    my_head = lax.axis_index("head")
    my_seq = lax.axis_index("seq")
    devices = heads_axis * seq_axis
    me = my_head * seq_axis + my_seq
    barrier = pltpu.get_barrier_semaphore()
    rows, width = latent_q.shape
    local_heads = rows // queries_count
    halves, _, half_rows = expo.shape
    half_queries = queries_count // halves
    tile = top_a.shape[1]
    tiles = rows // tile

    def place(index):
        return (index // seq_axis, lax.rem(index, seq_axis))

    loads = [pltpu.make_async_copy(turned_keys_hbm, turned_keys, load_sem.at[0])]
    for j in range(halves):
        part = pl.ds(j * half_rows, half_rows)
        loads.append(pltpu.make_async_copy(latent_q_hbm.at[part], latent_q.at[part], load_sem.at[1 + j]))
    loads.append(pltpu.make_async_copy(query_hbm, query_ref, load_sem.at[halves + 1]))
    loads.append(pltpu.make_async_copy(keys_hbm, keys_ref, load_sem.at[halves + 2]))
    loads.append(pltpu.make_async_copy(weight_hbm, weight_ref, load_sem.at[halves + 3]))
    for load in loads:
        load.start()

    def greet(offset, carry):
        other = lax.rem(me + offset, devices)
        pl.semaphore_signal(barrier, inc=1, device_id=place(other), device_id_type=MESH)
        return carry

    lax.fori_loop(1, devices, greet, 0)

    def stat_copy(half, offset, source, target):
        return pltpu.make_async_remote_copy(
            src_ref=stat_all.at[source, half],
            dst_ref=stat_all.at[source, half],
            send_sem=stat_send_sem.at[offset, half],
            recv_sem=stat_recv_sem.at[source, half],
            device_id=(my_head, target),
            device_id_type=MESH,
        )

    def stat_start(half):
        def start(offset, carry):
            stat_copy(half, offset, my_seq, lax.rem(my_seq + offset, seq_axis)).start()
            return carry

        lax.fori_loop(1, seq_axis, start, 0)

    def stat_wait(half):
        def wait(offset, carry):
            other = lax.rem(my_seq + offset, seq_axis)
            stat_copy(half, offset, other, other).wait_recv()
            return carry

        lax.fori_loop(1, seq_axis, wait, 0)

    def stat_sent(half):
        def sent(offset, carry):
            stat_copy(half, offset, my_seq, lax.rem(my_seq + offset, seq_axis)).wait_send()
            return carry

        lax.fori_loop(1, seq_axis, sent, 0)

    loads[0].wait()
    latent_keys[...] = turned_keys[...].T
    loads[1].wait()
    buffers = [(scores_a, top_a), (scores_b, top_b)]

    def multiply(t):
        buffer, top = buffers[t % 2]
        scores = lax.dot_general(
            latent_keys[...], latent_q[pl.ds(t * tile, tile), :], NT, preferred_element_type=F32
        )
        buffer[...] = scores
        top[...] = jnp.max(scores, axis=0, keepdims=True)

    def soften(t):
        buffer, top_ref = buffers[t % 2]
        top = top_ref[...]
        part = jnp.exp2((buffer[...] - top) * exponent_scale)
        half = t * tile // half_rows
        start = t * tile - half * half_rows
        expo[half, :, start : start + tile] = part.astype(BF16)
        total = jnp.sum(part, axis=0, keepdims=True)
        scaled = top * exponent_scale
        joint = scaled + jnp.log2(total)
        for j in range(tile // 128):
            row = start // 128 + j
            base[half, row : row + 1, :] = scaled[:, j * 128 : (j + 1) * 128]
            stat_all[my_seq, half, row : row + 1, :] = joint[:, j * 128 : (j + 1) * 128]

    early = (tiles * 3) // 4
    for t in range(tiles):
        if t * tile == half_rows:
            for j in range(2, halves + 1):
                loads[j].wait()
        multiply(t)
        if t:
            soften(t - 1)
        if t == early:
            pl.semaphore_wait(barrier, devices - 1)
            stat_start(0)
    soften(tiles - 1)
    stat_start(1)

    def index_copy(offset, source, target):
        return pltpu.make_async_remote_copy(
            src_ref=index_all.at[source],
            dst_ref=index_all.at[source],
            send_sem=index_send_sem.at[offset],
            recv_sem=index_recv_sem.at[source],
            device_id=place(target),
            device_id_type=MESH,
        )

    def index_start(offset, carry):
        index_copy(offset, me, lax.rem(me + offset, devices)).start()
        return carry

    def index_wait(offset, carry):
        other = lax.rem(me + offset, devices)
        index_copy(offset, other, other).wait_recv()
        return carry

    def index_sent(offset, carry):
        index_copy(offset, me, lax.rem(me + offset, devices)).wait_send()
        return carry

    for j in range(3):
        loads[halves + 1 + j].wait()
    blocks, block, _ = weights.shape
    fine = keys_ref.shape[0]
    group = math.gcd(blocks, 8)
    heads_in_block = block // queries_count
    wide = weight_ref[...].astype(F32)
    flat_queries[...] = query_ref[...].astype(F32)
    index_heads = wide.shape[1]
    for g in range(wide.shape[1]):
        row = g % heads_in_block * queries_count
        weights[g // heads_in_block, row : row + queries_count, :] = wide[:, g : g + 1]
        picked = flat_queries[pl.ds(g, queries_count, stride=index_heads), :]
        idx_q[g // heads_in_block, row : row + queries_count, :] = picked.astype(BF16)

    def index_scores(i, logits):
        queries = idx_q[pl.ds(i * group, group)]
        part = lax.dot_general(
            queries.reshape(group * block, -1), keys_ref[...], NT, preferred_element_type=F32
        )
        part = part.reshape(group, block, fine)
        act[pl.ds(i * group, group)] = part
        weighted = weights[pl.ds(i * group, group)] * jnp.maximum(part, 0.0)
        return logits + jnp.sum(
            weighted.reshape(group * heads_in_block, queries_count, fine), axis=0
        )

    logits = lax.fori_loop(
        0, blocks // group, index_scores, jnp.zeros((queries_count, fine), F32)
    )
    index_top = jnp.max(logits, axis=1, keepdims=True)
    index_total = jnp.sum(jnp.exp(logits - index_top), axis=1, keepdims=True)
    index_all[me] = to_row(index_top + jnp.log(index_total))
    lax.fori_loop(1, devices, index_start, 0)

    def sum_copy(half, offset, block_index, slot, target):
        return pltpu.make_async_remote_copy(
            src_ref=sum_send.at[block_index, half],
            dst_ref=sum_recv.at[slot, half],
            send_sem=sum_send_sem.at[offset, half],
            recv_sem=sum_recv_sem.at[slot, half],
            device_id=(target, my_seq),
            device_id_type=MESH,
        )

    def combine(half, target):
        mine = expo[half, pl.ds(pl.multiple_of(target * fine, fine), fine), :]
        both = lax.dot_general(spread[half], mine, NT, preferred_element_type=F32)
        return both[0:half_queries] + both[half_queries : 2 * half_queries]

    own_parts = []
    for half in range(halves):
        stat_wait(half)
        factor = jnp.exp2(base[half] - join_log2(stat_all[:, half]))
        upper = factor.astype(BF16).astype(F32)
        lower = factor - upper
        first = lax.broadcasted_iota(jnp.int32, (half_queries, 128), 0) * local_heads
        for j in range(half_rows // 128):
            lane = lax.broadcasted_iota(jnp.int32, (half_queries, 128), 1) + j * 128
            inside = jnp.logical_and(lane >= first, lane < first + local_heads)
            columns = slice(j * 128, (j + 1) * 128)
            spread[half, 0:half_queries, columns] = jnp.where(
                inside, upper[j : j + 1, :], 0.0
            ).astype(BF16)
            spread[half, half_queries : 2 * half_queries, columns] = jnp.where(
                inside, lower[j : j + 1, :], 0.0
            ).astype(BF16)
        for offset in range(1, heads_axis):
            target = lax.rem(my_head + offset, heads_axis)
            sum_send[target, half] = combine(half, target)
            sum_copy(half, offset, target, my_head, target).start()
        own_parts.append(combine(half, my_head))

    for half in range(halves):
        for offset in range(1, heads_axis):
            source = lax.rem(my_head + offset, heads_axis)
            sum_copy(half, offset, source, source, source).wait_recv()
            own_parts[half] = own_parts[half] + sum_recv[source, half]
    targets = jnp.concatenate(own_parts, axis=0) / heads
    lax.fori_loop(1, devices, index_wait, 0)
    index_log = to_column(join_log(index_all[...]), queries_count)
    shifted = logits - index_log
    positive = targets > 0
    own_loss = jnp.where(positive, targets * jnp.log(jnp.where(positive, targets, 1.0)), 0.0)
    own_loss = jnp.sum(own_loss - targets * shifted, axis=0, keepdims=True)
    own_loss = sum(own_loss[:, i * 128 : (i + 1) * 128] for i in range(fine // 128))
    grad = jnp.exp(shifted) - targets
    loss_all[me] = own_loss

    def loss_copy(offset, slot, target):
        return pltpu.make_async_remote_copy(
            src_ref=loss_all.at[slot],
            dst_ref=loss_all.at[slot],
            send_sem=loss_send_sem.at[offset],
            recv_sem=loss_recv_sem.at[slot],
            device_id=place(target),
            device_id_type=MESH,
        )

    chunk = own_term.shape[1]
    owners = block // chunk
    depth, peers = term_a.shape[0:2]
    inner = seq_axis // depth
    lanes = inner // 2
    my_depth = my_seq // inner
    my_inner = lax.rem(my_seq, inner)
    parity = lax.rem(my_seq, 2)
    pair = my_seq + 1 - 2 * parity
    my_peer = my_head * lanes + my_inner // 2

    def peer_at(offset):
        return lax.rem(my_peer + offset, peers)

    def depth_at(distance):
        return lax.rem(my_depth + distance, depth)

    def owner_of(layer, peer, side):
        return (peer // lanes) * seq_axis + layer * inner + 2 * lax.rem(peer, lanes) + side

    def pair_copy(layer, peer, side):
        owner = owner_of(layer, peer, side)
        return pltpu.make_async_remote_copy(
            src_ref=own_term.at[owner],
            dst_ref=pair_recv.at[owner],
            send_sem=pair_send_sem.at[layer, peer],
            recv_sem=pair_recv_sem.at[layer, peer],
            device_id=(my_head, pair),
            device_id_type=MESH,
        )

    def plane_copy(layer, source_slot, slot, target):
        return pltpu.make_async_remote_copy(
            src_ref=term_a.at[layer, source_slot],
            dst_ref=recv_a.at[layer, slot],
            send_sem=a_send_sem.at[layer, source_slot],
            recv_sem=a_recv_sem.at[layer, slot],
            device_id=(target // lanes, my_depth * inner + 2 * lax.rem(target, lanes) + parity),
            device_id_type=MESH,
        )

    def depth_copy(source_slot, slot, target):
        return pltpu.make_async_remote_copy(
            src_ref=term_b.at[source_slot],
            dst_ref=recv_b.at[slot],
            send_sem=b_send_sem.at[source_slot],
            recv_sem=b_recv_sem.at[slot],
            device_id=(my_head, target * inner + my_inner),
            device_id_type=MESH,
        )

    grads = jnp.concatenate([grad] * heads_in_block, axis=0)
    grad_upper = grads.astype(BF16).astype(F32)
    grad_lower = grads - grad_upper

    def back(chosen):
        upper_parts, lower_parts = [], []
        for b in chosen:
            part = act[b]
            on = part > 0
            dact[b] = jnp.where(on, grads * weights[b], 0.0).astype(BF16)
            upper_parts.append(jnp.where(on, grad_upper, 0.0).astype(BF16))
            lower_parts.append(jnp.where(on, grad_lower, 0.0).astype(BF16))
        both = jnp.concatenate(upper_parts + lower_parts, axis=0)
        result = jnp.dot(both, keys_ref[...], preferred_element_type=F32)
        result = result[0 : block * len(chosen)] + result[block * len(chosen) :]
        for i, b in enumerate(chosen):
            for j in range(owners):
                start = i * block + j * chunk
                own_term[b * owners + j] = result[start : start + chunk]

    def pair_start(distance):
        for offset in range(peers):
            pair_copy(depth_at(distance), peer_at(offset), 1 - parity).start()

    def plane_start(distance):
        layer = depth_at(distance)
        for offset in range(1, peers):
            peer = peer_at(offset)
            owner = owner_of(layer, peer, parity)
            pair_copy(layer, peer, parity).wait_recv()
            term_a[layer, peer] = (own_term[owner] + pair_recv[owner]).astype(BF16)
            plane_copy(layer, peer, my_peer, peer).start()
        pair_copy(layer, my_peer, parity).wait_recv()

    def layer_order(step):
        return lax.rem(step + 1, depth)

    if owners == 1:

        def first_half(step, carry):
            distance = layer_order(step)
            layer = depth_at(distance)
            back([owner_of(layer, peer_at(offset), 1 - parity) for offset in range(peers)])
            pair_start(distance)
            return carry

        def second_half(step, carry):
            distance = layer_order(step)
            layer = depth_at(distance)
            back([owner_of(layer, peer_at(offset), parity) for offset in range(peers)])
            plane_start(distance)
            return carry

    else:

        def every_block(b, carry):
            back([b])
            return carry

        def first_half(step, carry):
            pair_start(layer_order(step))
            return carry

        def second_half(step, carry):
            plane_start(layer_order(step))
            return carry

        lax.fori_loop(0, blocks, every_block, 0)

    lax.fori_loop(0, depth, first_half, 0)
    lax.fori_loop(0, depth, second_half, 0)

    def loss_start(offset, carry):
        loss_copy(offset, me, lax.rem(me + offset, devices)).start()
        return carry

    lax.fori_loop(1, devices, loss_start, 0)

    key_out[...] = lax.dot_general(
        dact[...].reshape(blocks * block, fine),
        idx_q[...].reshape(blocks * block, -1),
        TN,
        preferred_element_type=F32,
    )

    for half in range(halves):
        stat_sent(half)
        for offset in range(1, heads_axis):
            target = lax.rem(my_head + offset, heads_axis)
            sum_copy(half, offset, target, my_head, target).wait_send()
    lax.fori_loop(1, devices, index_sent, 0)

    def pair_sent(step, carry):
        for offset in range(peers):
            pair_copy(step, peer_at(offset), 1 - parity).wait_send()
        return carry

    lax.fori_loop(0, depth, pair_sent, 0)

    def plane_total(layer):
        owner = owner_of(layer, my_peer, parity)
        total = own_term[owner] + pair_recv[owner]
        for offset in range(1, peers):
            source = peer_at(offset)
            plane_copy(layer, source, source, source).wait_recv()
            total = total + recv_a[layer, source].astype(F32)
        return total

    def depth_start(distance, carry):
        layer = depth_at(distance)
        term_b[layer] = plane_total(layer).astype(BF16)
        depth_copy(layer, my_depth, layer).start()
        return carry

    lax.fori_loop(1, depth, depth_start, 0)

    def depth_wait(distance, total):
        source = depth_at(distance)
        depth_copy(source, source, source).wait_recv()
        return total + recv_b[source].astype(F32)

    total = lax.fori_loop(1, depth, depth_wait, plane_total(my_depth))
    own_block = me // owners
    inside_block = me - own_block * owners
    own_weights = weights[own_block]
    own_queries = idx_q[own_block].astype(F32)
    if owners == 1:
        query_out[...] = total * own_weights
        prod_out[...] = total * own_queries
    else:
        for j in range(owners):

            @pl.when(inside_block == j)
            def _():
                query_out[...] = total * own_weights[j * chunk : (j + 1) * chunk]
                prod_out[...] = total * own_queries[j * chunk : (j + 1) * chunk]

    def loss_wait(offset, carry):
        source = lax.rem(me + offset, devices)
        loss_copy(offset, source, source).wait_recv()
        return carry

    lax.fori_loop(1, devices, loss_wait, 0)
    loss_out[...] = jnp.sum(loss_all[...], axis=0)

    def last_sent(offset, carry):
        other = lax.rem(me + offset, devices)
        loss_copy(offset, me, other).wait_send()
        return carry

    def plane_sent(layer, carry):
        for offset in range(1, peers):
            plane_copy(layer, peer_at(offset), my_peer, peer_at(offset)).wait_send()
        return carry

    def depth_sent(distance, carry):
        layer = depth_at(distance)
        depth_copy(layer, my_depth, layer).wait_send()
        return carry

    lax.fori_loop(1, devices, last_sent, 0)
    lax.fori_loop(0, depth, plane_sent, 0)
    lax.fori_loop(1, depth, depth_sent, 0)


def closing(queries_count, loss_in, query_in, prod_in, key_in, loss_out, query_out, weight_out, key_out):
    loss_out[...] = jnp.sum(loss_in[...], axis=1, keepdims=True) / queries_count
    query_out[...] = query_in[...]
    ones = jnp.ones((8, prod_in.shape[1]), F32)
    sums = lax.dot_general(
        ones, prod_in[...], NT, precision=lax.Precision.HIGHEST, preferred_element_type=F32
    )
    weight_out[...] = sums[0:1]
    key_out[...] = key_in[...]


def shards(heads_axis, seq_axis, latent_q, latent_keys, idx_q, idx_keys, idx_weight):
    queries_count, local_heads, width = latent_q.shape
    index_heads, size = idx_q.shape[1:]
    rows = queries_count * local_heads
    keys = latent_keys.shape[0]
    fine = idx_keys.shape[1]
    devices = heads_axis * seq_axis
    all_rows = queries_count * index_heads
    chunk = all_rows // devices
    block = max(chunk, queries_count)
    blocks = all_rows // block
    halves = 2
    half_rows = rows // halves
    half_queries = queries_count // halves
    tile = min(256, half_rows)
    inner = math.gcd(seq_axis, 4)
    depth = seq_axis // inner
    peers = heads_axis * inner // 2
    queries = idx_q.reshape(all_rows, size)
    vmem = pl.BlockSpec(memory_space=pltpu.VMEM)
    dma = pltpu.SemaphoreType.DMA
    loss, query_grad, prod, key_grad = pl.pallas_call(
        functools.partial(
            kernel, heads_axis, seq_axis, local_heads * heads_axis, queries_count
        ),
        out_shape=(
            jax.ShapeDtypeStruct((1, 128), F32),
            jax.ShapeDtypeStruct((chunk, size), F32),
            jax.ShapeDtypeStruct((chunk, size), F32),
            jax.ShapeDtypeStruct((fine, size), F32),
        ),
        in_specs=[pl.BlockSpec(memory_space=pl.ANY)] * 5,
        out_specs=(vmem,) * 4,
        scratch_shapes=[
            pltpu.VMEM((rows, width), BF16),
            pltpu.VMEM((width, keys), BF16),
            pltpu.VMEM((all_rows, size), BF16),
            pltpu.VMEM((fine, size), BF16),
            pltpu.VMEM((queries_count, index_heads), BF16),
            dma((halves + 4,)),
            pltpu.VMEM((keys, width), BF16),
            pltpu.VMEM((keys, tile), F32),
            pltpu.VMEM((keys, tile), F32),
            pltpu.VMEM((1, tile), F32),
            pltpu.VMEM((1, tile), F32),
            pltpu.VMEM((blocks, block, size), BF16),
            pltpu.VMEM((all_rows, size), F32),
            pltpu.VMEM((blocks, block, 1), F32),
            pltpu.VMEM((devices, chunk, size), F32),
            pltpu.VMEM((devices, chunk, size), F32),
            pltpu.VMEM((devices, 1, 128), F32),
            pltpu.VMEM((halves, keys, half_rows), BF16),
            pltpu.VMEM((halves, half_rows // 128, 128), F32),
            pltpu.VMEM((halves, 2 * half_queries, half_rows), BF16),
            pltpu.VMEM((seq_axis, halves, half_rows // 128, 128), F32),
            pltpu.VMEM((heads_axis, halves, half_queries, fine), F32),
            pltpu.VMEM((heads_axis, halves, half_queries, fine), F32),
            pltpu.VMEM((blocks, block, fine), F32),
            pltpu.VMEM((blocks, block, fine), BF16),
            pltpu.VMEM((depth, peers, chunk, size), BF16),
            pltpu.VMEM((depth, peers, chunk, size), BF16),
            pltpu.VMEM((depth, chunk, size), BF16),
            pltpu.VMEM((depth, chunk, size), BF16),
            pltpu.VMEM((devices, 1, 128), F32),
            dma((seq_axis, halves)),
            dma((seq_axis, halves)),
            dma((heads_axis, halves)),
            dma((heads_axis, halves)),
            dma((depth, peers)),
            dma((depth, peers)),
            dma((depth,)),
            dma((depth,)),
            dma((devices,)),
            dma((devices,)),
            dma((depth, peers)),
            dma((depth, peers)),
            dma((devices,)),
            dma((devices,)),
        ],
        compiler_params=pltpu.CompilerParams(
            collective_id=0, has_side_effects=True, vmem_limit_bytes=60 * 1024 * 1024
        ),
    )(latent_q.reshape(rows, width), latent_keys.T, queries, idx_keys[0], idx_weight)
    loss, query_grad, weight_grad, key_grad = pl.pallas_call(
        functools.partial(closing, queries_count),
        out_shape=(
            jax.ShapeDtypeStruct((1, 1), F32),
            jax.ShapeDtypeStruct((chunk, size), F32),
            jax.ShapeDtypeStruct((1, chunk), F32),
            jax.ShapeDtypeStruct((fine, size), F32),
        ),
        in_specs=[vmem] * 4,
        out_specs=(vmem,) * 4,
    )(loss, query_grad, prod, key_grad)
    return (loss.reshape(()), query_grad, weight_grad.reshape(-1), key_grad[None])


def solution(mesh):
    in_specs = (P(None, "head", None), P("seq", None), P(), P("seq", "head", None), P())
    out_specs = (P(), P(("head", "seq"), None), P(("head", "seq")), P("seq", "head", None))
    body = functools.partial(shards, mesh.shape["head"], mesh.shape["seq"])
    return jax.shard_map(body, mesh=mesh, in_specs=in_specs, out_specs=out_specs, check_vma=False)
```

time: 42.5 us -> 34.7 us (0.82)
  Pallas kernels: 41.7 us -> 33.9 us
    pallas_call x1, Pallas kernels: 39.9 us -> 32.2 us  [shards(): pl.pallas_call(functools.partial(kernel, heads_axis, seq_axis, local_head...]
where the time goes in v1:
time: 34.7 us; the launch traced here: 34.6 us
  Pallas kernels  33.9 us (98%)
  between operations  0.64 us (2%)
    pallas_call x1, Pallas kernels, shards(): pl.pallas_call(functools.partial(kernel, heads_axis, seq_axis, local_head...  32.2 us
    pallas_call x1, Pallas kernels, shards(): pl.pallas_call(functools.partial(closing, queries_count), out_shape=(jax....  1.78 us

profile of v1, /device:TPU:0, one launch (start us, length us, event | category | flops | bytes accessed | tf_op | source)
XLA Modules:
  0.0 34.6 jit_solution(9150742460408181792)
XLA Ops:
  0.6 32.2 %shard_map.84 = (f32[1,128]{1,0:T(1,128)}, f32[64,128]{1,0:T(8,128)}, f32[64,128]{1,0:T(8,128)}, f32[512,128]{1,0:T(8,128)}) custom-call(bf16[2048,576]{1,0:T(8,128)(2,1)} %bitcast.7, bf16[576,1024]{1,0:T(8,128)(2,1)} %bitcast.8, bf16[2048,128]{1,0:T(8,128)(2,1)} %bitcast.9, bf16[512,128]{1,0:T(8,128)(2,1)} %bitcast.10, bf16[32,64]{1,0:T(8,128)(2,1)} %weight_hbm.1), custom_call_target="tpu_custom_call" | custom-call | tf_op jit(solution)/shard_map/pallas_call | solution.py:526
  32.8 1.8 %shard_map.85 = (f32[1,1]{1,0:T(1,128)}, f32[64,128]{1,0:T(8,128)}, f32[1,64]{1,0:T(1,128)}, f32[512,128]{1,0:T(8,128)}) custom-call(f32[1,128]{1,0:T(1,128)} %get-tuple-element.12.loss_in, f32[64,128]{1,0:T(8,128)} %get-tuple-element.13.query_in, f32[64,128]{1,0:T(8,128)} %get-tuple-element.14.prod_in, f32[512,128]{1,0:T(8,128)} %get-tuple-element.15.key_in), custom_call_target="tpu_custom_call" | custom-call | tf_op jit(solution)/shard_map/pallas_call | solution.py:588

commit v2 on v1

--- a/solution.py
+++ b/solution.py
@@ -79,37 +79,25 @@
 
     lax.fori_loop(1, devices, greet, 0)
 
-    def stat_copy(half, offset, source, target):
-        return pltpu.make_async_remote_copy(
-            src_ref=stat_all.at[source, half],
-            dst_ref=stat_all.at[source, half],
-            send_sem=stat_send_sem.at[offset, half],
-            recv_sem=stat_recv_sem.at[source, half],
+    def stat_copy(half, slots, target):
+        return pltpu.make_async_remote_copy(
+            src_ref=stat_all.at[half, slots],
+            dst_ref=stat_all.at[half, slots],
+            send_sem=stat_send_sem.at[half],
+            recv_sem=stat_recv_sem.at[half],
             device_id=(my_head, target),
             device_id_type=MESH,
         )
 
     def stat_start(half):
         def start(offset, carry):
-            stat_copy(half, offset, my_seq, lax.rem(my_seq + offset, seq_axis)).start()
+            stat_copy(half, my_seq, lax.rem(my_seq + offset, seq_axis)).start()
             return carry
 
         lax.fori_loop(1, seq_axis, start, 0)
 
-    def stat_wait(half):
-        def wait(offset, carry):
-            other = lax.rem(my_seq + offset, seq_axis)
-            stat_copy(half, offset, other, other).wait_recv()
-            return carry
-
-        lax.fori_loop(1, seq_axis, wait, 0)
-
-    def stat_sent(half):
-        def sent(offset, carry):
-            stat_copy(half, offset, my_seq, lax.rem(my_seq + offset, seq_axis)).wait_send()
-            return carry
-
-        lax.fori_loop(1, seq_axis, sent, 0)
+    other_seqs = pl.ds(0, seq_axis - 1)
+    other_devices = pl.ds(0, devices - 1)
 
     loads[0].wait()
     latent_keys[...] = turned_keys[...].T
@@ -137,14 +125,33 @@
         for j in range(tile // 128):
             row = start // 128 + j
             base[half, row : row + 1, :] = scaled[:, j * 128 : (j + 1) * 128]
-            stat_all[my_seq, half, row : row + 1, :] = joint[:, j * 128 : (j + 1) * 128]
+            stat_all[half, my_seq, row : row + 1, :] = joint[:, j * 128 : (j + 1) * 128]
+
+    blocks, block, _ = weights.shape
+    fine = keys_ref.shape[0]
+    group = math.gcd(blocks, 8)
+    heads_in_block = block // queries_count
+    index_heads = weight_ref.shape[1]
+
+    def reorder(g):
+        row = g % heads_in_block * queries_count
+        weights[g // heads_in_block, row : row + queries_count, :] = weight_ref[:, g : g + 1].astype(F32)
+        picked = flat_queries[pl.ds(g, queries_count, stride=index_heads), :]
+        idx_q[g // heads_in_block, row : row + queries_count, :] = picked.astype(BF16)
 
     early = (tiles * 3) // 4
+    late = tiles // 2
+    share = index_heads // (tiles - late)
     for t in range(tiles):
         if t * tile == half_rows:
-            for j in range(2, halves + 1):
-                loads[j].wait()
+            for load in loads[2:]:
+                load.wait()
         multiply(t)
+        if t == late:
+            flat_queries[...] = query_ref[...].astype(F32)
+        if t >= late:
+            for g in range((t - late) * share, index_heads if t == tiles - 1 else (t - late + 1) * share):
+                reorder(g)
         if t:
             soften(t - 1)
         if t == early:
@@ -153,43 +160,19 @@
     soften(tiles - 1)
     stat_start(1)
 
-    def index_copy(offset, source, target):
-        return pltpu.make_async_remote_copy(
-            src_ref=index_all.at[source],
-            dst_ref=index_all.at[source],
-            send_sem=index_send_sem.at[offset],
-            recv_sem=index_recv_sem.at[source],
+    def index_copy(slots, target):
+        return pltpu.make_async_remote_copy(
+            src_ref=index_all.at[slots],
+            dst_ref=index_all.at[slots],
+            send_sem=index_send_sem.at[0],
+            recv_sem=index_recv_sem.at[0],
             device_id=place(target),
             device_id_type=MESH,
         )
 
     def index_start(offset, carry):
-        index_copy(offset, me, lax.rem(me + offset, devices)).start()
+        index_copy(me, lax.rem(me + offset, devices)).start()
         return carry
-
-    def index_wait(offset, carry):
-        other = lax.rem(me + offset, devices)
-        index_copy(offset, other, other).wait_recv()
-        return carry
-
-    def index_sent(offset, carry):
-        index_copy(offset, me, lax.rem(me + offset, devices)).wait_send()
-        return carry
-
-    for j in range(3):
-        loads[halves + 1 + j].wait()
-    blocks, block, _ = weights.shape
-    fine = keys_ref.shape[0]
-    group = math.gcd(blocks, 8)
-    heads_in_block = block // queries_count
-    wide = weight_ref[...].astype(F32)
-    flat_queries[...] = query_ref[...].astype(F32)
-    index_heads = wide.shape[1]
-    for g in range(wide.shape[1]):
-        row = g % heads_in_block * queries_count
-        weights[g // heads_in_block, row : row + queries_count, :] = wide[:, g : g + 1]
-        picked = flat_queries[pl.ds(g, queries_count, stride=index_heads), :]
-        idx_q[g // heads_in_block, row : row + queries_count, :] = picked.astype(BF16)
 
     def index_scores(i, logits):
         queries = idx_q[pl.ds(i * group, group)]
@@ -211,15 +194,17 @@
     index_all[me] = to_row(index_top + jnp.log(index_total))
     lax.fori_loop(1, devices, index_start, 0)
 
-    def sum_copy(half, offset, block_index, slot, target):
-        return pltpu.make_async_remote_copy(
-            src_ref=sum_send.at[block_index, half],
-            dst_ref=sum_recv.at[slot, half],
-            send_sem=sum_send_sem.at[offset, half],
-            recv_sem=sum_recv_sem.at[slot, half],
+    def sum_copy(half, sources, slots, target):
+        return pltpu.make_async_remote_copy(
+            src_ref=sum_send.at[half, sources],
+            dst_ref=sum_recv.at[half, slots],
+            send_sem=sum_send_sem.at[half],
+            recv_sem=sum_recv_sem.at[half],
             device_id=(target, my_seq),
             device_id_type=MESH,
         )
+
+    other_heads = pl.ds(0, heads_axis - 1)
 
     def combine(half, target):
         mine = expo[half, pl.ds(pl.multiple_of(target * fine, fine), fine), :]
@@ -228,8 +213,8 @@
 
     own_parts = []
     for half in range(halves):
-        stat_wait(half)
-        factor = jnp.exp2(base[half] - join_log2(stat_all[:, half]))
+        stat_copy(half, other_seqs, my_seq).wait_recv()
+        factor = jnp.exp2(base[half] - join_log2(stat_all[half]))
         upper = factor.astype(BF16).astype(F32)
         lower = factor - upper
         first = lax.broadcasted_iota(jnp.int32, (half_queries, 128), 0) * local_heads
@@ -245,17 +230,17 @@
             ).astype(BF16)
         for offset in range(1, heads_axis):
             target = lax.rem(my_head + offset, heads_axis)
-            sum_send[target, half] = combine(half, target)
-            sum_copy(half, offset, target, my_head, target).start()
+            sum_send[half, target] = combine(half, target)
+            sum_copy(half, target, my_head, target).start()
         own_parts.append(combine(half, my_head))
 
     for half in range(halves):
+        sum_copy(half, other_heads, other_heads, my_head).wait_recv()
         for offset in range(1, heads_axis):
             source = lax.rem(my_head + offset, heads_axis)
-            sum_copy(half, offset, source, source, source).wait_recv()
-            own_parts[half] = own_parts[half] + sum_recv[source, half]
+            own_parts[half] = own_parts[half] + sum_recv[half, source]
     targets = jnp.concatenate(own_parts, axis=0) / heads
-    lax.fori_loop(1, devices, index_wait, 0)
+    index_copy(other_devices, me).wait_recv()
     index_log = to_column(join_log(index_all[...]), queries_count)
     shifted = logits - index_log
     positive = targets > 0
@@ -265,12 +250,12 @@
     grad = jnp.exp(shifted) - targets
     loss_all[me] = own_loss
 
-    def loss_copy(offset, slot, target):
-        return pltpu.make_async_remote_copy(
-            src_ref=loss_all.at[slot],
-            dst_ref=loss_all.at[slot],
-            send_sem=loss_send_sem.at[offset],
-            recv_sem=loss_recv_sem.at[slot],
+    def loss_copy(slots, target):
+        return pltpu.make_async_remote_copy(
+            src_ref=loss_all.at[slots],
+            dst_ref=loss_all.at[slots],
+            send_sem=loss_send_sem.at[0],
+            recv_sem=loss_recv_sem.at[0],
             device_id=place(target),
             device_id_type=MESH,
         )
@@ -295,33 +280,36 @@
     def owner_of(layer, peer, side):
         return (peer // lanes) * seq_axis + layer * inner + 2 * lax.rem(peer, lanes) + side
 
-    def pair_copy(layer, peer, side):
-        owner = owner_of(layer, peer, side)
-        return pltpu.make_async_remote_copy(
-            src_ref=own_term.at[owner],
-            dst_ref=pair_recv.at[owner],
-            send_sem=pair_send_sem.at[layer, peer],
-            recv_sem=pair_recv_sem.at[layer, peer],
+    every_peer = pl.ds(0, peers)
+    other_peers = pl.ds(0, peers - 1)
+    other_layers = pl.ds(0, depth - 1)
+
+    def pair_copy(layer, slots):
+        return pltpu.make_async_remote_copy(
+            src_ref=own_term.at[slots],
+            dst_ref=pair_recv.at[slots],
+            send_sem=pair_send_sem.at[0],
+            recv_sem=pair_recv_sem.at[layer],
             device_id=(my_head, pair),
             device_id_type=MESH,
         )
 
-    def plane_copy(layer, source_slot, slot, target):
-        return pltpu.make_async_remote_copy(
-            src_ref=term_a.at[layer, source_slot],
-            dst_ref=recv_a.at[layer, slot],
-            send_sem=a_send_sem.at[layer, source_slot],
-            recv_sem=a_recv_sem.at[layer, slot],
+    def plane_copy(layer, sources, slots, target):
+        return pltpu.make_async_remote_copy(
+            src_ref=term_a.at[layer, sources],
+            dst_ref=recv_a.at[layer, slots],
+            send_sem=a_send_sem.at[layer],
+            recv_sem=a_recv_sem.at[layer],
             device_id=(target // lanes, my_depth * inner + 2 * lax.rem(target, lanes) + parity),
             device_id_type=MESH,
         )
 
-    def depth_copy(source_slot, slot, target):
-        return pltpu.make_async_remote_copy(
-            src_ref=term_b.at[source_slot],
-            dst_ref=recv_b.at[slot],
-            send_sem=b_send_sem.at[source_slot],
-            recv_sem=b_recv_sem.at[slot],
+    def depth_copy(sources, slots, target):
+        return pltpu.make_async_remote_copy(
+            src_ref=term_b.at[sources],
+            dst_ref=recv_b.at[slots],
+            send_sem=b_send_sem.at[0],
+            recv_sem=b_recv_sem.at[0],
             device_id=(my_head, target * inner + my_inner),
             device_id_type=MESH,
         )
@@ -346,60 +334,54 @@
                 start = i * block + j * chunk
                 own_term[b * owners + j] = result[start : start + chunk]
 
-    def pair_start(distance):
+    def layer_at(step):
+        up = step + jnp.where(step >= my_depth, 1, 0)
+        down = depth - 1 - step
+        down = down - jnp.where(down <= my_depth, 1, 0)
+        return jnp.where(step >= depth - 1, my_depth, jnp.where(2 * my_depth >= depth, up, down))
+
+    def pair_start(layer):
         for offset in range(peers):
-            pair_copy(depth_at(distance), peer_at(offset), 1 - parity).start()
-
-    def plane_start(distance):
-        layer = depth_at(distance)
+            pair_copy(layer, owner_of(layer, peer_at(offset), 1 - parity)).start()
+
+    def plane_start(layer):
+        pair_copy(layer, every_peer).wait_recv()
         for offset in range(1, peers):
             peer = peer_at(offset)
             owner = owner_of(layer, peer, parity)
-            pair_copy(layer, peer, parity).wait_recv()
             term_a[layer, peer] = (own_term[owner] + pair_recv[owner]).astype(BF16)
             plane_copy(layer, peer, my_peer, peer).start()
-        pair_copy(layer, my_peer, parity).wait_recv()
-
-    def layer_order(step):
-        return lax.rem(step + 1, depth)
-
-    if owners == 1:
-
-        def first_half(step, carry):
-            distance = layer_order(step)
-            layer = depth_at(distance)
-            back([owner_of(layer, peer_at(offset), 1 - parity) for offset in range(peers)])
-            pair_start(distance)
-            return carry
-
-        def second_half(step, carry):
-            distance = layer_order(step)
-            layer = depth_at(distance)
-            back([owner_of(layer, peer_at(offset), parity) for offset in range(peers)])
-            plane_start(distance)
-            return carry
-
-    else:
+
+    def layer_back(layer, side):
+        if owners == 1:
+            back([owner_of(layer, peer_at(offset), side) for offset in range(peers)])
+
+    if owners > 1:
 
         def every_block(b, carry):
             back([b])
             return carry
 
-        def first_half(step, carry):
-            pair_start(layer_order(step))
-            return carry
-
-        def second_half(step, carry):
-            plane_start(layer_order(step))
-            return carry
-
         lax.fori_loop(0, blocks, every_block, 0)
 
-    lax.fori_loop(0, depth, first_half, 0)
-    lax.fori_loop(0, depth, second_half, 0)
+    layer_back(layer_at(0), 1 - parity)
+    pair_start(layer_at(0))
+
+    def mixed(step, carry):
+        ahead = layer_at(step + 1)
+        layer_back(ahead, 1 - parity)
+        pair_start(ahead)
+        layer = layer_at(step)
+        layer_back(layer, parity)
+        plane_start(layer)
+        return carry
+
+    lax.fori_loop(0, depth - 1, mixed, 0)
+    layer_back(my_depth, parity)
+    plane_start(my_depth)
 
     def loss_start(offset, carry):
-        loss_copy(offset, me, lax.rem(me + offset, devices)).start()
+        loss_copy(me, lax.rem(me + offset, devices)).start()
         return carry
 
     lax.fori_loop(1, devices, loss_start, 0)
@@ -412,42 +394,32 @@
     )
 
     for half in range(halves):
-        stat_sent(half)
-        for offset in range(1, heads_axis):
-            target = lax.rem(my_head + offset, heads_axis)
-            sum_copy(half, offset, target, my_head, target).wait_send()
-    lax.fori_loop(1, devices, index_sent, 0)
-
-    def pair_sent(step, carry):
-        for offset in range(peers):
-            pair_copy(step, peer_at(offset), 1 - parity).wait_send()
-        return carry
-
-    lax.fori_loop(0, depth, pair_sent, 0)
+        stat_copy(half, other_seqs, my_seq).wait_send()
+        sum_copy(half, other_heads, other_heads, my_head).wait_send()
+    index_copy(other_devices, me).wait_send()
+
+    pair_copy(0, pl.ds(0, depth * peers)).wait_send()
 
     def plane_total(layer):
         owner = owner_of(layer, my_peer, parity)
+        plane_copy(layer, other_peers, other_peers, my_peer).wait_recv()
         total = own_term[owner] + pair_recv[owner]
         for offset in range(1, peers):
-            source = peer_at(offset)
-            plane_copy(layer, source, source, source).wait_recv()
-            total = total + recv_a[layer, source].astype(F32)
+            total = total + recv_a[layer, peer_at(offset)].astype(F32)
         return total
 
-    def depth_start(distance, carry):
-        layer = depth_at(distance)
+    def depth_start(step, carry):
+        layer = layer_at(step)
         term_b[layer] = plane_total(layer).astype(BF16)
         depth_copy(layer, my_depth, layer).start()
         return carry
 
-    lax.fori_loop(1, depth, depth_start, 0)
-
-    def depth_wait(distance, total):
-        source = depth_at(distance)
-        depth_copy(source, source, source).wait_recv()
-        return total + recv_b[source].astype(F32)
-
-    total = lax.fori_loop(1, depth, depth_wait, plane_total(my_depth))
+    lax.fori_loop(0, depth - 1, depth_start, 0)
+    total = plane_total(my_depth)
+    if depth > 1:
+        depth_copy(other_layers, other_layers, my_depth).wait_recv()
+    for distance in range(1, depth):
+        total = total + recv_b[depth_at(distance)].astype(F32)
     own_block = me // owners
     inside_block = me - own_block * owners
     own_weights = weights[own_block]
@@ -463,32 +435,17 @@
                 query_out[...] = total * own_weights[j * chunk : (j + 1) * chunk]
                 prod_out[...] = total * own_queries[j * chunk : (j + 1) * chunk]
 
-    def loss_wait(offset, carry):
-        source = lax.rem(me + offset, devices)
-        loss_copy(offset, source, source).wait_recv()
+    loss_copy(other_devices, me).wait_recv()
+    loss_out[...] = jnp.sum(loss_all[...], axis=0)
+    loss_copy(other_devices, me).wait_send()
+
+    def plane_sent(layer, carry):
+        plane_copy(layer, other_peers, other_peers, my_peer).wait_send()
         return carry
 
-    lax.fori_loop(1, devices, loss_wait, 0)
-    loss_out[...] = jnp.sum(loss_all[...], axis=0)
-
-    def last_sent(offset, carry):
-        other = lax.rem(me + offset, devices)
-        loss_copy(offset, me, other).wait_send()
-        return carry
-
-    def plane_sent(layer, carry):
-        for offset in range(1, peers):
-            plane_copy(layer, peer_at(offset), my_peer, peer_at(offset)).wait_send()
-        return carry
-
-    def depth_sent(distance, carry):
-        layer = depth_at(distance)
-        depth_copy(layer, my_depth, layer).wait_send()
-        return carry
-
-    lax.fori_loop(1, devices, last_sent, 0)
     lax.fori_loop(0, depth, plane_sent, 0)
-    lax.fori_loop(1, depth, depth_sent, 0)
+    if depth > 1:
+        depth_copy(other_layers, other_layers, my_depth).wait_send()
 
 
 def closing(queries_count, loss_in, query_in, prod_in, key_in, loss_out, query_out, weight_out, key_out):
@@ -556,9 +513,9 @@
             pltpu.VMEM((halves, keys, half_rows), BF16),
             pltpu.VMEM((halves, half_rows // 128, 128), F32),
             pltpu.VMEM((halves, 2 * half_queries, half_rows), BF16),
-            pltpu.VMEM((seq_axis, halves, half_rows // 128, 128), F32),
-            pltpu.VMEM((heads_axis, halves, half_queries, fine), F32),
-            pltpu.VMEM((heads_axis, halves, half_queries, fine), F32),
+            pltpu.VMEM((halves, seq_axis, half_rows // 128, 128), F32),
+            pltpu.VMEM((halves, heads_axis, half_queries, fine), F32),
+            pltpu.VMEM((halves, heads_axis, half_queries, fine), F32),
             pltpu.VMEM((blocks, block, fine), F32),
             pltpu.VMEM((blocks, block, fine), BF16),
             pltpu.VMEM((depth, peers, chunk, size), BF16),
@@ -566,20 +523,20 @@
             pltpu.VMEM((depth, chunk, size), BF16),
             pltpu.VMEM((depth, chunk, size), BF16),
             pltpu.VMEM((devices, 1, 128), F32),
-            dma((seq_axis, halves)),
-            dma((seq_axis, halves)),
-            dma((heads_axis, halves)),
-            dma((heads_axis, halves)),
-            dma((depth, peers)),
-            dma((depth, peers)),
+            dma((halves,)),
+            dma((halves,)),
+            dma((halves,)),
+            dma((halves,)),
             dma((depth,)),
             dma((depth,)),
-            dma((devices,)),
-            dma((devices,)),
-            dma((depth, peers)),
-            dma((depth, peers)),
-            dma((devices,)),
-            dma((devices,)),
+            dma((1,)),
+            dma((1,)),
+            dma((1,)),
+            dma((1,)),
+            dma((1,)),
+            dma((depth,)),
+            dma((1,)),
+            dma((1,)),
         ],
         compiler_params=pltpu.CompilerParams(
             collective_id=0, has_side_effects=True, vmem_limit_bytes=60 * 1024 * 1024

time: 34.7 us -> 32.2 us (0.928)
  Pallas kernels: 33.9 us -> 31.4 us
    pallas_call x1, Pallas kernels: 32.2 us -> 29.6 us  [shards(): pl.pallas_call(functools.partial(kernel, heads_axis, seq_axis, local_head...]
where the time goes in v2:
time: 32.2 us; the launch traced here: 32 us
  Pallas kernels  31.4 us (98%)
  between operations  0.64 us (2%)
    pallas_call x1, Pallas kernels, shards(): pl.pallas_call(functools.partial(kernel, heads_axis, seq_axis, local_head...  29.6 us
    pallas_call x1, Pallas kernels, shards(): pl.pallas_call(functools.partial(closing, queries_count), out_shape=(jax....  1.78 us

profile of v2, /device:TPU:0, one launch (start us, length us, event | category | flops | bytes accessed | tf_op | source)
XLA Modules:
  0.0 32.0 jit_solution(15436049532935838385)
XLA Ops:
  0.6 29.6 %shard_map.84 = (f32[1,128]{1,0:T(1,128)}, f32[64,128]{1,0:T(8,128)}, f32[64,128]{1,0:T(8,128)}, f32[512,128]{1,0:T(8,128)}) custom-call(bf16[2048,576]{1,0:T(8,128)(2,1)} %bitcast.7, bf16[576,1024]{1,0:T(8,128)(2,1)} %bitcast.8, bf16[2048,128]{1,0:T(8,128)(2,1)} %bitcast.9, bf16[512,128]{1,0:T(8,128)(2,1)} %bitcast.10, bf16[32,64]{1,0:T(8,128)(2,1)} %weight_hbm.1), custom_call_target="tpu_custom_call" | custom-call | tf_op jit(solution)/shard_map/pallas_call | solution.py:483
  30.2 1.8 %shard_map.85 = (f32[1,1]{1,0:T(1,128)}, f32[64,128]{1,0:T(8,128)}, f32[1,64]{1,0:T(1,128)}, f32[512,128]{1,0:T(8,128)}) custom-call(f32[1,128]{1,0:T(1,128)} %get-tuple-element.12.loss_in, f32[64,128]{1,0:T(8,128)} %get-tuple-element.13.query_in, f32[64,128]{1,0:T(8,128)} %get-tuple-element.14.prod_in, f32[512,128]{1,0:T(8,128)} %get-tuple-element.15.key_in), custom_call_target="tpu_custom_call" | custom-call | tf_op jit(solution)/shard_map/pallas_call | solution.py:545

commit v3 on v2

--- a/solution.py
+++ b/solution.py
@@ -139,7 +139,7 @@
         picked = flat_queries[pl.ds(g, queries_count, stride=index_heads), :]
         idx_q[g // heads_in_block, row : row + queries_count, :] = picked.astype(BF16)
 
-    early = (tiles * 3) // 4
+    early = (tiles * 5) // 8
     late = tiles // 2
     share = index_heads // (tiles - late)
     for t in range(tiles):
@@ -448,15 +448,21 @@
         depth_copy(other_layers, other_layers, my_depth).wait_send()
 
 
-def closing(queries_count, loss_in, query_in, prod_in, key_in, loss_out, query_out, weight_out, key_out):
+def closing(queries_count, loss_in, query_in, prod_in, key_in, loss_out, query_out, weight_out, key_out, sems):
+    copies = [
+        pltpu.make_async_copy(key_in, key_out, sems.at[0]),
+        pltpu.make_async_copy(query_in, query_out, sems.at[1]),
+    ]
+    for copy in copies:
+        copy.start()
     loss_out[...] = jnp.sum(loss_in[...], axis=1, keepdims=True) / queries_count
-    query_out[...] = query_in[...]
     ones = jnp.ones((8, prod_in.shape[1]), F32)
     sums = lax.dot_general(
         ones, prod_in[...], NT, precision=lax.Precision.HIGHEST, preferred_element_type=F32
     )
     weight_out[...] = sums[0:1]
-    key_out[...] = key_in[...]
+    for copy in copies:
+        copy.wait()
 
 
 def shards(heads_axis, seq_axis, latent_q, latent_keys, idx_q, idx_keys, idx_weight):
@@ -485,12 +491,12 @@
             kernel, heads_axis, seq_axis, local_heads * heads_axis, queries_count
         ),
         out_shape=(
-            jax.ShapeDtypeStruct((1, 128), F32),
-            jax.ShapeDtypeStruct((chunk, size), F32),
-            jax.ShapeDtypeStruct((chunk, size), F32),
-            jax.ShapeDtypeStruct((fine, size), F32),
+            pltpu.VMEM((1, 128), F32),
+            pltpu.VMEM((chunk, size), F32),
+            pltpu.VMEM((chunk, size), F32),
+            pltpu.VMEM((fine, size), F32),
         ),
-        in_specs=[pl.BlockSpec(memory_space=pl.ANY)] * 5,
+        in_specs=[pl.BlockSpec(memory_space=pltpu.HBM)] * 5,
         out_specs=(vmem,) * 4,
         scratch_shapes=[
             pltpu.VMEM((rows, width), BF16),
@@ -539,9 +545,14 @@
             dma((1,)),
         ],
         compiler_params=pltpu.CompilerParams(
-            collective_id=0, has_side_effects=True, vmem_limit_bytes=60 * 1024 * 1024
+            collective_id=0, has_side_effects=True, vmem_limit_bytes=56 * 1024 * 1024
         ),
     )(latent_q.reshape(rows, width), latent_keys.T, queries, idx_keys[0], idx_weight)
+    held = [
+        pltpu.with_memory_space_constraint(x, pltpu.VMEM)
+        for x in (loss, query_grad, prod, key_grad)
+    ]
+    hbm = pl.BlockSpec(memory_space=pltpu.HBM)
     loss, query_grad, weight_grad, key_grad = pl.pallas_call(
         functools.partial(closing, queries_count),
         out_shape=(
@@ -551,8 +562,9 @@
             jax.ShapeDtypeStruct((fine, size), F32),
         ),
         in_specs=[vmem] * 4,
-        out_specs=(vmem,) * 4,
-    )(loss, query_grad, prod, key_grad)
+        out_specs=(vmem, hbm, vmem, hbm),
+        scratch_shapes=[dma((2,))],
+    )(*held)
     return (loss.reshape(()), query_grad, weight_grad.reshape(-1), key_grad[None])
 
 

time: 32.2 us -> 30.2 us (0.938)
  Pallas kernels: 31.4 us -> 29.4 us
    pallas_call x1, Pallas kernels: 29.6 us -> 28.2 us  [shards(): pl.pallas_call(functools.partial(kernel, heads_axis, seq_axis, local_head...]
    pallas_call x1, Pallas kernels: 1.78 us -> 1.24 us  [shards(): pl.pallas_call(functools.partial(closing, queries_count), out_shape=(jax....]
where the time goes in v3:
time: 30.2 us; the launch traced here: 30.1 us
  Pallas kernels  29.4 us (97%)
  between operations  0.64 us (2%)
    pallas_call x1, Pallas kernels, shards(): pl.pallas_call(functools.partial(kernel, heads_axis, seq_axis, local_head...  28.2 us
    pallas_call x1, Pallas kernels, shards(): pl.pallas_call(functools.partial(closing, queries_count), out_shape=(jax....  1.24 us

profile of v3, /device:TPU:0, one launch (start us, length us, event | category | flops | bytes accessed | tf_op | source)
XLA Modules:
  0.0 30.1 jit_solution(17301312267915037012)
XLA Ops:
  0.6 28.2 %shard_map.84 = (f32[1,128]{1,0:T(1,128)S(1)}, f32[64,128]{1,0:T(8,128)S(1)}, f32[64,128]{1,0:T(8,128)S(1)}, f32[512,128]{1,0:T(8,128)S(1)}) custom-call(bf16[2048,576]{1,0:T(8,128)(2,1)} %bitcast.7, bf16[576,1024]{1,0:T(8,128)(2,1)} %bitcast.8, bf16[2048,128]{1,0:T(8,128)(2,1)} %bitcast.9, bf16[512,128]{1,0:T(8,128)(2,1)} %bitcast.10, bf16[32,64]{1,0:T(8,128)(2,1)} %weight_hbm.1), custom_call_target="tpu_custom_call" | custom-call | tf_op jit(solution)/shard_map/pallas_call | solution.py:489
  28.8 1.2 %shard_map.85 = (f32[1,1]{1,0:T(1,128)}, f32[64,128]{1,0:T(8,128)}, f32[1,64]{1,0:T(1,128)}, f32[512,128]{1,0:T(8,128)}) custom-call(f32[1,128]{1,0:T(1,128)S(1)} %get-tuple-element.12.loss_in, f32[64,128]{1,0:T(8,128)S(1)} %get-tuple-element.13.query_in, f32[64,128]{1,0:T(8,128)S(1)} %get-tuple-element.14.prod_in, f32[512,128]{1,0:T(8,128)S(1)} %get-tuple-element.15.key_in), custom_call_target="tpu_custom_call" | custom-call | tf_op jit(solution)/shard_map/pallas_call | solution.py:556

commit v4 on v3

--- a/solution.py
+++ b/solution.py
@@ -69,7 +69,7 @@
     loads.append(pltpu.make_async_copy(query_hbm, query_ref, load_sem.at[halves + 1]))
     loads.append(pltpu.make_async_copy(keys_hbm, keys_ref, load_sem.at[halves + 2]))
     loads.append(pltpu.make_async_copy(weight_hbm, weight_ref, load_sem.at[halves + 3]))
-    for load in loads:
+    for load in loads[:2]:
         load.start()
 
     def greet(offset, carry):
@@ -78,6 +78,8 @@
         return carry
 
     lax.fori_loop(1, devices, greet, 0)
+    for load in loads[2:]:
+        load.start()
 
     def stat_copy(half, slots, target):
         return pltpu.make_async_remote_copy(
@@ -367,6 +369,11 @@
     layer_back(layer_at(0), 1 - parity)
     pair_start(layer_at(0))
 
+    def loss_start(offset, carry):
+        loss_copy(me, lax.rem(me + offset, devices)).start()
+        return carry
+
+
     def mixed(step, carry):
         ahead = layer_at(step + 1)
         layer_back(ahead, 1 - parity)
@@ -377,14 +384,9 @@
         return carry
 
     lax.fori_loop(0, depth - 1, mixed, 0)
+    lax.fori_loop(1, devices, loss_start, 0)
     layer_back(my_depth, parity)
     plane_start(my_depth)
-
-    def loss_start(offset, carry):
-        loss_copy(me, lax.rem(me + offset, devices)).start()
-        return carry
-
-    lax.fori_loop(1, devices, loss_start, 0)
 
     key_out[...] = lax.dot_general(
         dact[...].reshape(blocks * block, fine),

time: 30.2 us -> 30.1 us (level)
  no operation moved by 1% of the time
where the time goes in v4:
time: 30.1 us; the launch traced here: 30 us
  Pallas kernels  29.3 us (97%)
  between operations  0.64 us (2%)
    pallas_call x1, Pallas kernels, shards(): pl.pallas_call(functools.partial(kernel, heads_axis, seq_axis, local_head...  28.1 us
    pallas_call x1, Pallas kernels, shards(): pl.pallas_call(functools.partial(closing, queries_count), out_shape=(jax....  1.24 us

profile of v4, /device:TPU:0, one launch (start us, length us, event | category | flops | bytes accessed | tf_op | source)
XLA Modules:
  0.0 30.0 jit_solution(10203524140129675478)
XLA Ops:
  0.6 28.1 %shard_map.84 = (f32[1,128]{1,0:T(1,128)S(1)}, f32[64,128]{1,0:T(8,128)S(1)}, f32[64,128]{1,0:T(8,128)S(1)}, f32[512,128]{1,0:T(8,128)S(1)}) custom-call(bf16[2048,576]{1,0:T(8,128)(2,1)} %bitcast.7, bf16[576,1024]{1,0:T(8,128)(2,1)} %bitcast.8, bf16[2048,128]{1,0:T(8,128)(2,1)} %bitcast.9, bf16[512,128]{1,0:T(8,128)(2,1)} %bitcast.10, bf16[32,64]{1,0:T(8,128)(2,1)} %weight_hbm.1), custom_call_target="tpu_custom_call" | custom-call | tf_op jit(solution)/shard_map/pallas_call | solution.py:491
  28.7 1.2 %shard_map.85 = (f32[1,1]{1,0:T(1,128)}, f32[64,128]{1,0:T(8,128)}, f32[1,64]{1,0:T(1,128)}, f32[512,128]{1,0:T(8,128)}) custom-call(f32[1,128]{1,0:T(1,128)S(1)} %get-tuple-element.12.loss_in, f32[64,128]{1,0:T(8,128)S(1)} %get-tuple-element.13.query_in, f32[64,128]{1,0:T(8,128)S(1)} %get-tuple-element.14.prod_in, f32[512,128]{1,0:T(8,128)S(1)} %get-tuple-element.15.key_in), custom_call_target="tpu_custom_call" | custom-call | tf_op jit(solution)/shard_map/pallas_call | solution.py:558
